TPU v7x, 32 devices: a whole 2x2x4 slice. The times are simulated.
32 devices in a mesh: phase: 2 (over core), dp: 8 (over z, y), mp: 2 (over x).
Axes of the slice: x: 2, y: 2, z: 4, core: 2. Of those that a mesh axis runs over, the one named last changes fastest.
Arguments:
- segments: bfloat16 [2, 16, 64, 4096], P(None, 'dp', 'mp'), may hold values from -6 to 6
- memory_in: bfloat16 [16, 64, 4096], P('dp', 'mp'), may hold values from -6 to 6
- seg_lengths: int32 [2, 16], P(None, 'dp'), may hold values from 1 to 64, as said below
- routes: int32 [2, 8], replicated, may hold values from 0 to 7, each once within a row
- w_query: bfloat16 [2, 4096, 4096], P('phase', None, 'mp'), may hold values from -12 to 12
- w_key: bfloat16 [2, 4096, 1024], P('phase', None, 'mp'), may hold values from -1 to 1
- value_weight: bfloat16 [2, 4096, 1024], P('phase', None, 'mp'), may hold values from -0.09375 to 0.09375
- w_out: bfloat16 [2, 4096, 4096], P('phase', 'mp'), may hold values from -0.09375 to 0.09375
- norm_gain: bfloat16 [2, 4096], P('phase'), may hold values from 0.099609375 to 1.8984375
Outputs:
- mem_states: bfloat16 [2, 2, 16, 64, 4096], P('phase', None, 'dp', 'mp')
- seg_states: bfloat16 [2, 2, 16, 64, 4096], P('phase', None, 'dp', 'mp')
Inputs may be any that keep to these rules, and one draw needn't show every extreme that they name: Each row m is a permutation of the data groups: slot m of group g hands its memory to slot m of group routes[m, g]. `seg_lengths`: some entry equals 64.
All inputs are finite; a program needn't handle non-finite values.
Results may differ from a plain program's by a relative error of at most 0.025.
Values may be sent and summed in bfloat16 or wider, within the bound.
No kernel may reach another device: no remote copies, remote signals or barrier semaphores. Data moves between devices by JAX's collectives and lax.ppermute only.
A program may use at most 192 MiB of HBM per device.

v0:
```python
import jax
import jax.numpy as jnp
from jax import lax
from jax.sharding import PartitionSpec as P

HEAD_SIZE = 128
EPSILON = 1e-05


def shifted(value, axis, steps):
    count = lax.axis_size(axis)
    pairs = [(source, (source + steps) % count) for source in range(count)]
    return lax.ppermute(value, axis, pairs)


def norm_rows(rows, gain):
    values = rows.astype(jnp.float32)
    scaled = values * lax.rsqrt(jnp.mean(values * values, axis=-1, keepdims=True) + EPSILON)
    return (scaled * gain.astype(jnp.float32)).astype(jnp.bfloat16)


def section_layer(mem_x, seg_x, length, w_query, w_key, value_weight, w_out, gain):
    mem_dev = mem_x.shape[0]
    seg_dev = seg_x.shape[0]
    raw_mem, raw_seg = (
        lax.all_gather(mem_x, "mp", axis=0, tiled=True),
        lax.all_gather(seg_x, "mp", axis=0, tiled=True),
    )
    all_mem = norm_rows(raw_mem, gain)
    all_seg = norm_rows(raw_seg, gain)
    mem_rows = all_mem.shape[0]
    normed = jnp.concatenate([all_mem, all_seg], axis=0)
    rows_total = normed.shape[0]
    kv_dev = w_key.shape[1] // HEAD_SIZE
    query_dev = w_query.shape[1] // HEAD_SIZE
    per_group = query_dev // kv_dev
    heads_of_query = jnp.dot(normed, w_query, preferred_element_type=jnp.float32).astype(
        jnp.bfloat16
    )
    heads_of_query = heads_of_query.reshape(rows_total, kv_dev, per_group, HEAD_SIZE)
    heads_of_key = jnp.dot(normed, w_key, preferred_element_type=jnp.float32).astype(jnp.bfloat16)
    heads_of_key = heads_of_key.reshape(rows_total, kv_dev, HEAD_SIZE)
    heads_of_value = jnp.dot(normed, value_weight, preferred_element_type=jnp.float32).astype(
        jnp.bfloat16
    )
    heads_of_value = heads_of_value.reshape(rows_total, kv_dev, HEAD_SIZE)
    scores = jnp.einsum(
        "qcgd,kcd->cgqk", heads_of_query, heads_of_key, preferred_element_type=jnp.float32
    ) * HEAD_SIZE ** (-0.5)
    query_pos = lax.broadcasted_iota(jnp.int32, (rows_total, rows_total), 0)
    key_pos = lax.broadcasted_iota(jnp.int32, (rows_total, rows_total), 1)
    visible = (key_pos < mem_rows) | (key_pos - mem_rows < length) & (
        (query_pos < mem_rows) | (key_pos <= query_pos)
    )
    scores = jnp.where(visible, scores, -1e30)
    row_max = jnp.max(scores, axis=-1, keepdims=True)
    exponent = jnp.exp(scores - row_max)
    attn = (exponent / jnp.sum(exponent, axis=-1, keepdims=True)).astype(jnp.bfloat16)
    attended = jnp.einsum(
        "cgqk,kcd->qcgd", attn, heads_of_value, preferred_element_type=jnp.float32
    )
    attended = attended.astype(jnp.bfloat16).reshape(rows_total, query_dev * HEAD_SIZE)
    attended_mem = attended[:mem_rows]
    attended_seg = attended[mem_rows:]
    block_rows = mem_dev + seg_dev
    blocks = block_rows * lax.axis_size("mp") // block_rows
    term_mem = jnp.dot(attended_mem, w_out, preferred_element_type=jnp.float32).reshape(
        blocks, mem_dev, -1
    )
    term_seg = jnp.dot(attended_seg, w_out, preferred_element_type=jnp.float32).reshape(
        blocks, seg_dev, -1
    )
    summed = lax.psum_scatter(
        jnp.concatenate([term_mem, term_seg], axis=1)
        .reshape(block_rows * lax.axis_size("mp"), -1)
        .astype(jnp.bfloat16),
        "mp",
        scatter_dimension=0,
        tiled=True,
    ).astype(jnp.float32)
    new_mem = (mem_x.astype(jnp.float32) + summed[:mem_dev]).astype(jnp.bfloat16)
    new_seg = (seg_x.astype(jnp.float32) + summed[mem_dev:]).astype(jnp.bfloat16)
    return (new_mem, new_seg)


def route_memory(arrived, perm_row, group_index):
    group_count = perm_row.shape[0]
    group_ids = jnp.arange(group_count, dtype=jnp.int32)
    target = jnp.sum(jnp.where(group_ids == group_index, perm_row, 0))
    outgoing = jnp.where(
        (group_ids == target)[:, None, None], arrived[None], jnp.zeros_like(arrived)[None]
    )
    received = lax.all_to_all(outgoing, "dp", split_axis=0, concat_axis=0, tiled=True)
    return jnp.sum(received.astype(jnp.float32), axis=0).astype(jnp.bfloat16)


def per_device(
    segments, memory_in, seg_lengths, routes, w_query, w_key, value_weight, w_out, norm_gain
):
    rounds = segments.shape[0]
    slot_count = memory_in.shape[0]
    phase_count = lax.axis_size("phase")
    step_count = rounds * slot_count + phase_count - 1
    phase_index = lax.axis_index("phase")
    group_index = lax.axis_index("dp")
    is_first = phase_index == 0
    items = rounds * slot_count
    lengths_flat = seg_lengths.reshape(items)
    item_ids = jnp.arange(items, dtype=jnp.int32)
    mem_buf = jnp.where(is_first, memory_in[0], jnp.zeros_like(memory_in[0]))
    seg_buf = jnp.where(is_first, segments[0, 0], jnp.zeros_like(segments[0, 0]))
    mem_hist = jnp.zeros((items,) + memory_in.shape[1:], jnp.bfloat16)
    seg_hist = jnp.zeros((items,) + segments.shape[2:], jnp.bfloat16)
    for step in range(step_count):
        item_index = step - phase_index
        is_valid = (item_index >= 0) & (item_index < items)
        clipped = jnp.clip(item_index, 0, items - 1)
        length = jnp.sum(jnp.where(item_ids == clipped, lengths_flat, 0))
        mem_new, seg_new = section_layer(
            mem_buf, seg_buf, length, w_query[0], w_key[0], value_weight[0], w_out[0], norm_gain[0]
        )
        mem_current = lax.dynamic_index_in_dim(mem_hist, clipped, 0, keepdims=False)
        seg_current = lax.dynamic_index_in_dim(seg_hist, clipped, 0, keepdims=False)
        mem_hist = lax.dynamic_update_index_in_dim(
            mem_hist, jnp.where(is_valid, mem_new, mem_current), clipped, 0
        )
        seg_hist = lax.dynamic_update_index_in_dim(
            seg_hist, jnp.where(is_valid, seg_new, seg_current), clipped, 0
        )
        if step + 1 < step_count:
            mem_pass, seg_pass = shifted((mem_new, seg_new), "phase", 1)
            next_item = step + 1
            if next_item < items:
                next_round, next_slot = divmod(next_item, slot_count)
                if next_round == 0:
                    first_mem = memory_in[next_slot]
                else:
                    first_mem = route_memory(mem_pass, routes[next_slot], group_index)
                first_seg = segments[next_round, next_slot]
            else:
                first_mem = jnp.zeros_like(mem_pass)
                first_seg = jnp.zeros_like(seg_pass)
            mem_buf = jnp.where(is_first, first_mem, mem_pass)
            seg_buf = jnp.where(is_first, first_seg, seg_pass)
    mem_states = mem_hist.reshape((1, rounds, slot_count) + memory_in.shape[1:])
    seg_states = seg_hist.reshape((1, rounds, slot_count) + segments.shape[2:])
    return (mem_states, seg_states)


def solution(mesh):
    return jax.shard_map(
        per_device,
        mesh=mesh,
        in_specs=(
            P(None, "dp", "mp", None),
            P("dp", "mp", None),
            P(None, "dp"),
            P(),
            P("phase", None, "mp"),
            P("phase", None, "mp"),
            P("phase", None, "mp"),
            P("phase", "mp", None),
            P("phase", None),
        ),
        out_specs=(P("phase", None, "dp", "mp", None), P("phase", None, "dp", "mp", None)),
        check_vma=False,
    )
```

profile of v0, /device:TPU:0, one launch (start us, length us, event | category | flops | bytes accessed | tf_op | source)
XLA Modules:
  0.0 495.5 jit_solution(5529236552270811867)
XLA Ops:
  7.3 1.6 fusion.256
  13.1 9.9 %all-gather.1 = bf16[1,1,64,4096]{3,2,1,0:T(8,128)(2,1)S(1)} all-gather(bf16[1,1,32,4096]{3,2,1,0:T(8,128)(2,1)S(1)} %slice_select_fusion), channel_id=3, replica_groups=mesh['phase'=2,'dp'=8,'mp'=2] {'mp'}, dimensions={2}, use_global_device_ids=true | all-gather | bytes 786432 | tf_op jit(solution)/shard_map/all_gather | solution.py:27
  24.2 8.1 %all-gather = bf16[1,64,4096]{2,1,0:T(8,128)(2,1)S(1)} all-gather(bf16[1,32,4096]{2,1,0:T(8,128)(2,1)S(1)} %slice_select_fusion.1), channel_id=2, replica_groups=mesh['phase'=2,'dp'=8,'mp'=2] {'mp'}, dimensions={1}, use_global_device_ids=true | all-gather | bytes 786432 | tf_op jit(solution)/shard_map/all_gather | solution.py:26
  34.5 8.1 %fusion.85 = bf16[128,2048]{1,0:T(8,128)(2,1)S(1)} fusion(bf16[1,4096,2048]{2,1,0:T(8,128)(2,1)} %param.13, bf16[64,4096]{1,0:T(8,128)(2,1)S(1)} %get-tuple-element.52, bf16[64,4096]{1,0:T(8,128)(2,1)S(1)} %get-tuple-element.51), kind=kOutput, calls=%fused_computation.65 | convolution fusion | flops 2149842944 | bytes 18350080 | tf_op jit(solution)/shard_map/dot_general | solution.py:37
  44.6 2.9 fusion.125
  48.8 8.8 %fusion.35 = bf16[2,32,4096]{2,1,0:T(8,128)(2,1)S(1)} fusion(bf16[2,32,2048]{2,1,0:T(8,128)(2,1)S(1)} %dot_general.130, bf16[1,2048,4096]{2,1,0:T(8,128)(2,1)} %param.16), kind=kOutput, calls=%fused_computation.35 | convolution fusion | flops 1074003968 | bytes 17563648 | tf_op jit(solution)/shard_map/dot_general | solution.py:67
  57.6 8.8 %fusion.38 = bf16[2,32,4096]{2,1,0:T(8,128)(2,1)S(1)} fusion(bf16[2,32,2048]{2,1,0:T(8,128)(2,1)S(1)} %dot_general.132, bf16[1,2048,4096]{2,1,0:T(8,128)(2,1)} %param.16), kind=kOutput, calls=%fused_computation.36 | convolution fusion | flops 1074003968 | bytes 17563648 | tf_op jit(solution)/shard_map/dot_general | solution.py:70
  67.5 9.4 %reduce-scatter.8.cloned.1.call-start = ((), (), s32[]{:S(2)}) async-start(), calls=%async_computation.8 | async-start | bytes 1572864 | tf_op jit(solution)/shard_map/reduce_scatter | solution.py:73
  77.0 12.3 %reduce-scatter.6.cloned.1.call-done = bf16[64,4096]{1,0:T(8,128)(2,1)} async-done(((bf16[128,4096]{1,0:T(8,128)(2,1)}), bf16[64,4096]{1,0:T(8,128)(2,1)}) %reduce-scatter.6.cloned.1.call-update) | async-done | bytes 524304 | tf_op jit(solution)/shard_map/reduce_scatter | solution.py:73
  90.8 1.2 bitcast_dynamic-update-slice_fusion.3
  92.7 8.9 %all_gather.32 = bf16[64,4096]{1,0:T(8,128)(2,1)S(1)} all-gather(bf16[32,4096]{1,0:T(8,128)(2,1)S(1)} %bitcast_select_fusion.9), channel_id=1, replica_groups=mesh['phase'=2,'dp'=8,'mp'=2] {'mp'}, dimensions={0}, use_global_device_ids=true | all-gather | bytes 786432 | tf_op jit(solution)/shard_map/all_gather | solution.py:26
  102.8 8.0 %all_gather.33 = bf16[64,4096]{1,0:T(8,128)(2,1)S(1)} all-gather(bf16[32,4096]{1,0:T(8,128)(2,1)S(1)} %bitcast_select_fusion.8), channel_id=1, replica_groups=mesh['phase'=2,'dp'=8,'mp'=2] {'mp'}, dimensions={0}, use_global_device_ids=true | all-gather | bytes 786432 | tf_op jit(solution)/shard_map/all_gather | solution.py:27
  112.2 8.3 %fusion.88 = bf16[128,2048]{1,0:T(8,128)(2,1)S(1)} fusion(bf16[1,4096,2048]{2,1,0:T(8,128)(2,1)} %param.13, bf16[64,4096]{1,0:T(8,128)(2,1)S(1)} %get-tuple-element.50, bf16[64,4096]{1,0:T(8,128)(2,1)S(1)} %get-tuple-element.49), kind=kOutput, calls=%fused_computation.66 | convolution fusion | flops 2149842944 | bytes 18350080 | tf_op jit(solution)/shard_map/dot_general | solution.py:37
  121.3 1.2 reshape.227
  122.5 2.3 fusion.117
  124.8 1.5 fusion.307
  126.4 2.0 fusion.121
  129.5 8.8 %fusion.41 = bf16[2,32,4096]{2,1,0:T(8,128)(2,1)S(1)} fusion(bf16[2,32,2048]{2,1,0:T(8,128)(2,1)S(1)} %dot_general.139, bf16[1,2048,4096]{2,1,0:T(8,128)(2,1)} %param.16), kind=kOutput, calls=%fused_computation.37 | convolution fusion | flops 1074003968 | bytes 17563648 | tf_op jit(solution)/shard_map/dot_general | solution.py:67
  140.4 8.8 %fusion.44 = bf16[2,32,4096]{2,1,0:T(8,128)(2,1)S(1)} fusion(bf16[2,32,2048]{2,1,0:T(8,128)(2,1)S(1)} %dot_general.141, bf16[1,2048,4096]{2,1,0:T(8,128)(2,1)} %param.16), kind=kOutput, calls=%fused_computation.38 | convolution fusion | flops 1074003968 | bytes 17563648 | tf_op jit(solution)/shard_map/dot_general | solution.py:70
  150.4 20.5 %reduce-scatter.8.cloned.1.call-done = bf16[64,4096]{1,0:T(8,128)(2,1)} async-done(((bf16[128,4096]{1,0:T(8,128)(2,1)}), bf16[64,4096]{1,0:T(8,128)(2,1)}) %reduce-scatter.8.cloned.1.call-update) | async-done | bytes 524304 | tf_op jit(solution)/shard_map/reduce_scatter | solution.py:73
  174.6 1.6 broadcast_select_fusion.1
  176.2 5.5 %all-to-all-start = ((bf16[8,32,4096]{2,1,0:T(8,128)(2,1)}), bf16[8,32,4096]{2,1,0:T(8,128)(2,1)S(1)}, u32[]{:S(2)}, u32[]{:S(2)}) async-start(bf16[8,32,4096]{2,1,0:T(8,128)(2,1)} %broadcast_select_fusion.1), calls=%async_computation.2 | async-start | bytes 4194304 | tf_op jit(solution)/shard_map/all_to_all | solution.py:93
  181.9 1.5 collective-permute-done.3
  184.4 9.0 %all_gather.35 = bf16[64,4096]{1,0:T(8,128)(2,1)S(1)} all-gather(bf16[32,4096]{1,0:T(8,128)(2,1)S(1)} %bitcast_select_fusion.6), channel_id=1, replica_groups=mesh['phase'=2,'dp'=8,'mp'=2] {'mp'}, dimensions={0}, use_global_device_ids=true | all-gather | bytes 786432 | tf_op jit(solution)/shard_map/all_gather | solution.py:27
  193.6 36.7 %all-to-all-done = bf16[8,32,4096]{2,1,0:T(8,128)(2,1)S(1)} async-done(((bf16[8,32,4096]{2,1,0:T(8,128)(2,1)}), bf16[8,32,4096]{2,1,0:T(8,128)(2,1)S(1)}, u32[]{:S(2)}, u32[]{:S(2)}) %all-to-all-start) | async-done | bytes 2097184 | tf_op jit(solution)/shard_map/all_to_all | solution.py:93
  230.7 8.1 %all_gather.34 = bf16[64,4096]{1,0:T(8,128)(2,1)S(1)} all-gather(bf16[32,4096]{1,0:T(8,128)(2,1)S(1)} %broadcast_select_fusion.5), channel_id=1, replica_groups=mesh['phase'=2,'dp'=8,'mp'=2] {'mp'}, dimensions={0}, use_global_device_ids=true | all-gather | bytes 786432 | tf_op jit(solution)/shard_map/all_gather | solution.py:26
  240.2 8.3 %fusion.91 = bf16[128,2048]{1,0:T(8,128)(2,1)S(1)} fusion(bf16[1,4096,2048]{2,1,0:T(8,128)(2,1)} %param.13, bf16[64,4096]{1,0:T(8,128)(2,1)S(1)} %get-tuple-element.48, bf16[64,4096]{1,0:T(8,128)(2,1)S(1)} %get-tuple-element.47), kind=kOutput, calls=%fused_computation.67 | convolution fusion | flops 2149842944 | bytes 18350080 | tf_op jit(solution)/shard_map/dot_general | solution.py:37
  251.4 8.8 %fusion.47 = bf16[2,32,4096]{2,1,0:T(8,128)(2,1)S(1)} fusion(bf16[2,32,2048]{2,1,0:T(8,128)(2,1)S(1)} %dot_general.148, bf16[1,2048,4096]{2,1,0:T(8,128)(2,1)} %param.16), kind=kOutput, calls=%fused_computation.39 | convolution fusion | flops 1074003968 | bytes 17563648 | tf_op jit(solution)/shard_map/dot_general | solution.py:67
  260.6 8.8 %fusion.50 = bf16[2,32,4096]{2,1,0:T(8,128)(2,1)S(1)} fusion(bf16[2,32,2048]{2,1,0:T(8,128)(2,1)S(1)} %dot_general.150, bf16[1,2048,4096]{2,1,0:T(8,128)(2,1)} %param.16), kind=kOutput, calls=%fused_computation.40 | convolution fusion | flops 1074003968 | bytes 17563648 | tf_op jit(solution)/shard_map/dot_general | solution.py:70
  272.4 17.6 %reduce-scatter.10.cloned.1.call-done = bf16[64,4096]{1,0:T(8,128)(2,1)} async-done(((bf16[128,4096]{1,0:T(8,128)(2,1)}), bf16[64,4096]{1,0:T(8,128)(2,1)}) %reduce-scatter.10.cloned.1.call-update) | async-done | bytes 524304 | tf_op jit(solution)/shard_map/reduce_scatter | solution.py:73
  293.7 1.6 broadcast_select_fusion
  295.3 5.5 %all-to-all-start.1 = ((bf16[8,32,4096]{2,1,0:T(8,128)(2,1)}), bf16[8,32,4096]{2,1,0:T(8,128)(2,1)S(1)}, u32[]{:S(2)}, u32[]{:S(2)}) async-start(bf16[8,32,4096]{2,1,0:T(8,128)(2,1)} %broadcast_select_fusion), calls=%async_computation.4 | async-start | bytes 4194304 | tf_op jit(solution)/shard_map/all_to_all | solution.py:93
  301.1 1.5 collective-permute-done.5
  303.6 9.0 %all_gather.37 = bf16[64,4096]{1,0:T(8,128)(2,1)S(1)} all-gather(bf16[32,4096]{1,0:T(8,128)(2,1)S(1)} %bitcast_select_fusion.4), channel_id=1, replica_groups=mesh['phase'=2,'dp'=8,'mp'=2] {'mp'}, dimensions={0}, use_global_device_ids=true | all-gather | bytes 786432 | tf_op jit(solution)/shard_map/all_gather | solution.py:27
  312.8 36.5 %all-to-all-done.1 = bf16[8,32,4096]{2,1,0:T(8,128)(2,1)S(1)} async-done(((bf16[8,32,4096]{2,1,0:T(8,128)(2,1)}), bf16[8,32,4096]{2,1,0:T(8,128)(2,1)S(1)}, u32[]{:S(2)}, u32[]{:S(2)}) %all-to-all-start.1) | async-done | bytes 2097184 | tf_op jit(solution)/shard_map/all_to_all | solution.py:93
  351.5 7.2 %all_gather.36 = bf16[64,4096]{1,0:T(8,128)(2,1)S(1)} all-gather(bf16[32,4096]{1,0:T(8,128)(2,1)S(1)} %broadcast_select_fusion.4), channel_id=1, replica_groups=mesh['phase'=2,'dp'=8,'mp'=2] {'mp'}, dimensions={0}, use_global_device_ids=true | all-gather | bytes 786432 | tf_op jit(solution)/shard_map/all_gather | solution.py:26
  360.0 8.3 %fusion.94 = bf16[128,2048]{1,0:T(8,128)(2,1)S(1)} fusion(bf16[1,4096,2048]{2,1,0:T(8,128)(2,1)} %param.13, bf16[64,4096]{1,0:T(8,128)(2,1)S(1)} %get-tuple-element.46, bf16[64,4096]{1,0:T(8,128)(2,1)S(1)} %get-tuple-element.45), kind=kOutput, calls=%fused_computation.68 | convolution fusion | flops 2149842944 | bytes 18350080 | tf_op jit(solution)/shard_map/dot_general | solution.py:37
  371.2 8.8 %fusion.53 = bf16[2,32,4096]{2,1,0:T(8,128)(2,1)S(1)} fusion(bf16[2,32,2048]{2,1,0:T(8,128)(2,1)S(1)} %dot_general.157, bf16[1,2048,4096]{2,1,0:T(8,128)(2,1)} %param.16), kind=kOutput, calls=%fused_computation.41 | convolution fusion | flops 1074003968 | bytes 17563648 | tf_op jit(solution)/shard_map/dot_general | solution.py:67
  380.5 8.9 %fusion.56 = bf16[2,32,4096]{2,1,0:T(8,128)(2,1)S(1)} fusion(bf16[2,32,2048]{2,1,0:T(8,128)(2,1)S(1)} %dot_general.159, bf16[1,2048,4096]{2,1,0:T(8,128)(2,1)} %param.16), kind=kOutput, calls=%fused_computation.42 | convolution fusion | flops 1074003968 | bytes 17563648 | tf_op jit(solution)/shard_map/dot_general | solution.py:70
  390.6 19.3 %reduce-scatter.12.cloned.1.call-done = bf16[64,4096]{1,0:T(8,128)(2,1)} async-done(((bf16[128,4096]{1,0:T(8,128)(2,1)}), bf16[64,4096]{1,0:T(8,128)(2,1)}) %reduce-scatter.12.cloned.1.call-update) | async-done | bytes 524304 | tf_op jit(solution)/shard_map/reduce_scatter | solution.py:73
  413.6 9.2 %all_gather.39 = bf16[64,4096]{1,0:T(8,128)(2,1)S(1)} all-gather(bf16[32,4096]{1,0:T(8,128)(2,1)S(1)} %broadcast_select_fusion.2), channel_id=1, replica_groups=mesh['phase'=2,'dp'=8,'mp'=2] {'mp'}, dimensions={0}, use_global_device_ids=true | all-gather | bytes 786432 | tf_op jit(solution)/shard_map/all_gather | solution.py:27
  423.1 8.2 %all_gather.38 = bf16[64,4096]{1,0:T(8,128)(2,1)S(1)} all-gather(bf16[32,4096]{1,0:T(8,128)(2,1)S(1)} %broadcast_select_fusion.3), channel_id=1, replica_groups=mesh['phase'=2,'dp'=8,'mp'=2] {'mp'}, dimensions={0}, use_global_device_ids=true | all-gather | bytes 786432 | tf_op jit(solution)/shard_map/all_gather | solution.py:26
  432.6 8.3 %fusion.97 = bf16[128,2048]{1,0:T(8,128)(2,1)S(1)} fusion(bf16[1,4096,2048]{2,1,0:T(8,128)(2,1)} %param.13, bf16[64,4096]{1,0:T(8,128)(2,1)S(1)} %get-tuple-element.44, bf16[64,4096]{1,0:T(8,128)(2,1)S(1)} %get-tuple-element.43), kind=kOutput, calls=%fused_computation.69 | convolution fusion | flops 2149842944 | bytes 18350080 | tf_op jit(solution)/shard_map/dot_general | solution.py:37
  442.1 1.3 fusion.111
  443.9 2.0 fusion.124
  446.3 8.8 %fusion.59 = bf16[2,32,4096]{2,1,0:T(8,128)(2,1)S(1)} fusion(bf16[2,32,2048]{2,1,0:T(8,128)(2,1)S(1)} %dot_general.166, bf16[1,2048,4096]{2,1,0:T(8,128)(2,1)} %param.16), kind=kOutput, calls=%fused_computation.43 | convolution fusion | flops 1074003968 | bytes 17563648 | tf_op jit(solution)/shard_map/dot_general | solution.py:67
  455.5 8.8 %fusion.62 = bf16[2,32,4096]{2,1,0:T(8,128)(2,1)S(1)} fusion(bf16[2,32,2048]{2,1,0:T(8,128)(2,1)S(1)} %dot_general.168, bf16[1,2048,4096]{2,1,0:T(8,128)(2,1)} %param.16), kind=kOutput, calls=%fused_computation.44 | convolution fusion | flops 1074003968 | bytes 17563648 | tf_op jit(solution)/shard_map/dot_general | solution.py:70
  465.5 20.5 %reduce-scatter.14.cloned.1.call-done = bf16[64,4096]{1,0:T(8,128)(2,1)} async-done(((bf16[128,4096]{1,0:T(8,128)(2,1)}), bf16[64,4096]{1,0:T(8,128)(2,1)}) %reduce-scatter.14.cloned.1.call-update) | async-done | bytes 524304 | tf_op jit(solution)/shard_map/reduce_scatter | solution.py:73
  (203 shorter events, 59.2 us)
Async XLA Ops:
  7.2 82.1 %reduce-scatter.6.cloned.1.call-start = ((), (), s32[]{:S(2)}) async-start(), calls=%async_computation.7 | async-start | bytes 1572864 | tf_op jit(solution)/shard_map/reduce_scatter | solution.py:73
  7.2 26.4 %copy-start.16 = (bf16[1,4096,512]{2,1,0:T(8,128)(2,1)S(1)}, bf16[1,4096,512]{2,1,0:T(8,128)(2,1)}, u32[]{:S(2)}) copy-start(bf16[1,4096,512]{2,1,0:T(8,128)(2,1)} %param.14) | copy-start | bytes 12582916
  66.4 24.1 %copy-start.6 = (bf16[2,32,4096]{2,1,0:T(8,128)(2,1)S(1)}, bf16[2,32,4096]{2,1,0:T(8,128)(2,1)}, u32[]{:S(2)}) copy-start(bf16[2,32,4096]{2,1,0:T(8,128)(2,1)} %param.10) | copy-start | bytes 1572868
  67.5 103.3 %reduce-scatter.8.cloned.1.call-start = ((), (), s32[]{:S(2)}) async-start(), calls=%async_computation.8 | async-start | bytes 1572864 | tf_op jit(solution)/shard_map/reduce_scatter | solution.py:73
  90.6 20.8 %copy-start.17 = (bf16[1,4096,512]{2,1,0:T(8,128)(2,1)S(1)}, bf16[1,4096,512]{2,1,0:T(8,128)(2,1)}, u32[]{:S(2)}) copy-start(bf16[1,4096,512]{2,1,0:T(8,128)(2,1)} %param.14) | copy-start | bytes 12582916
  90.6 2.0 collective-permute-start
  92.0 9.8 %collective-permute-start.1 = (bf16[32,4096]{1,0:T(8,128)(2,1)S(1)}, bf16[32,4096]{1,0:T(8,128)(2,1)S(1)}, u32[]{:S(2)}, u32[]{:S(2)}) collective-permute-start(bf16[32,4096]{1,0:T(8,128)(2,1)S(1)} %get-tuple-element.16), channel_id=1, source_target_pairs={{0,16},{16,0},{1,17},{17,1},{2,18},{18,2},{3,19},{19,3},{4,20},{20... | collective-permute-start | bytes 786440 | tf_op jit(solution)/shard_map/ppermute | solution.py:13
  112.2 8.4 %copy-start.21 = (bf16[1,4096,512]{2,1,0:T(8,128)(2,1)S(1)}, bf16[1,4096,512]{2,1,0:T(8,128)(2,1)}, u32[]{:S(2)}) copy-start(bf16[1,4096,512]{2,1,0:T(8,128)(2,1)} %param.15) | copy-start | bytes 12582916
  129.5 8.9 %copy-start.7 = (bf16[64,4,4,128]{3,0,2,1:T(8,128)(2,1)S(1)}, bf16[64,4,4,128]{3,0,2,1:T(8,128)(2,1)}, u32[]{:S(2)}) copy-start(bf16[64,4,4,128]{3,0,2,1:T(8,128)(2,1)} %get-tuple-element.40) | copy-start | bytes 786436
  149.2 23.7 %copy-start.15 = (s32[2,8]{1,0:T(2,128)S(1)}, s32[2,8]{1,0:T(2,128)}, u32[]{:S(2)}) copy-start(s32[2,8]{1,0:T(2,128)} %param.12) | copy-start | bytes 196
  172.9 3.3 copy-start
  172.9 3.3 copy-start.3
  172.9 1.7 collective-permute-start.2
  176.2 54.1 %all-to-all-start = ((bf16[8,32,4096]{2,1,0:T(8,128)(2,1)}), bf16[8,32,4096]{2,1,0:T(8,128)(2,1)S(1)}, u32[]{:S(2)}, u32[]{:S(2)}) async-start(bf16[8,32,4096]{2,1,0:T(8,128)(2,1)} %broadcast_select_fusion.1), calls=%async_computation.2 | async-start | bytes 4194304 | tf_op jit(solution)/shard_map/all_to_all | solution.py:93
  181.7 108.3 %reduce-scatter.10.cloned.1.call-start = ((), (), s32[]{:S(2)}) async-start(), calls=%async_computation.9 | async-start | bytes 1572864 | tf_op jit(solution)/shard_map/reduce_scatter | solution.py:73
  181.8 1.6 collective-permute-start.3
  230.7 8.7 %copy-start.18 = (bf16[1,4096,512]{2,1,0:T(8,128)(2,1)S(1)}, bf16[1,4096,512]{2,1,0:T(8,128)(2,1)}, u32[]{:S(2)}) copy-start(bf16[1,4096,512]{2,1,0:T(8,128)(2,1)} %param.14) | copy-start | bytes 12582916
  240.2 8.3 %copy-start.22 = (bf16[1,4096,512]{2,1,0:T(8,128)(2,1)S(1)}, bf16[1,4096,512]{2,1,0:T(8,128)(2,1)}, u32[]{:S(2)}) copy-start(bf16[1,4096,512]{2,1,0:T(8,128)(2,1)} %param.15) | copy-start | bytes 12582916
  248.5 1.1 copy-start.14
  292.2 1.5 collective-permute-start.4
  295.3 54.0 %all-to-all-start.1 = ((bf16[8,32,4096]{2,1,0:T(8,128)(2,1)}), bf16[8,32,4096]{2,1,0:T(8,128)(2,1)S(1)}, u32[]{:S(2)}, u32[]{:S(2)}) async-start(bf16[8,32,4096]{2,1,0:T(8,128)(2,1)} %broadcast_select_fusion), calls=%async_computation.4 | async-start | bytes 4194304 | tf_op jit(solution)/shard_map/all_to_all | solution.py:93
  300.8 109.1 %reduce-scatter.12.cloned.1.call-start = ((), (), s32[]{:S(2)}) async-start(), calls=%async_computation.10 | async-start | bytes 1572864 | tf_op jit(solution)/shard_map/reduce_scatter | solution.py:73
  301.0 1.6 collective-permute-start.5
  350.4 8.9 %copy-start.19 = (bf16[1,4096,512]{2,1,0:T(8,128)(2,1)S(1)}, bf16[1,4096,512]{2,1,0:T(8,128)(2,1)}, u32[]{:S(2)}) copy-start(bf16[1,4096,512]{2,1,0:T(8,128)(2,1)} %param.14) | copy-start | bytes 12582916
  360.0 8.3 %copy-start.23 = (bf16[1,4096,512]{2,1,0:T(8,128)(2,1)S(1)}, bf16[1,4096,512]{2,1,0:T(8,128)(2,1)}, u32[]{:S(2)}) copy-start(bf16[1,4096,512]{2,1,0:T(8,128)(2,1)} %param.15) | copy-start | bytes 12582916
  368.3 1.1 copy-start.13
  380.4 10.1 %copy-start.4 = (bf16[4,32,4096]{2,1,0:T(8,128)(2,1)S(1)}, bf16[4,32,4096]{2,1,0:T(8,128)(2,1)}, u32[]{:S(2)}) copy-start(bf16[4,32,4096]{2,1,0:T(8,128)(2,1)} %get-tuple-element.29) | copy-start | bytes 3145732
  380.4 10.1 %copy-start.1 = (bf16[4,32,4096]{2,1,0:T(8,128)(2,1)S(1)}, bf16[4,32,4096]{2,1,0:T(8,128)(2,1)}, u32[]{:S(2)}) copy-start(bf16[4,32,4096]{2,1,0:T(8,128)(2,1)} %get-tuple-element.11) | copy-start | bytes 3145732
  390.5 95.5 %reduce-scatter.14.cloned.1.call-start = ((), (), s32[]{:S(2)}) async-start(), calls=%async_computation.11 | async-start | bytes 1572864 | tf_op jit(solution)/shard_map/reduce_scatter | solution.py:73
  411.0 20.8 %copy-start.20 = (bf16[1,4096,512]{2,1,0:T(8,128)(2,1)S(1)}, bf16[1,4096,512]{2,1,0:T(8,128)(2,1)}, u32[]{:S(2)}) copy-start(bf16[1,4096,512]{2,1,0:T(8,128)(2,1)} %param.14) | copy-start | bytes 12582916
  411.2 1.6 collective-permute-start.7
  411.3 11.7 %collective-permute-start.6 = (bf16[32,4096]{1,0:T(8,128)(2,1)S(1)}, bf16[32,4096]{1,0:T(8,128)(2,1)S(1)}, u32[]{:S(2)}, u32[]{:S(2)}) collective-permute-start(bf16[32,4096]{1,0:T(8,128)(2,1)S(1)} %get-tuple-element.28), channel_id=1, source_target_pairs={{0,16},{16,0},{1,17},{17,1},{2,18},{18,2},{3,19},{19,3},{4,20},{20... | collective-permute-start | bytes 786440 | tf_op jit(solution)/shard_map/ppermute | solution.py:13
  412.8 0.7 copy-start.8
  423.0 8.4 %copy-start.10 = (bf16[32,4096]{1,0:T(8,128)(2,1)}, bf16[32,4096]{1,0:T(8,128)(2,1)S(1)}, u32[]{:S(2)}) copy-start(bf16[32,4096]{1,0:T(8,128)(2,1)S(1)} %collective-permute-done.6) | copy-start | bytes 786436
  432.6 8.4 %copy-start.24 = (bf16[1,4096,512]{2,1,0:T(8,128)(2,1)S(1)}, bf16[1,4096,512]{2,1,0:T(8,128)(2,1)}, u32[]{:S(2)}) copy-start(bf16[1,4096,512]{2,1,0:T(8,128)(2,1)} %param.15) | copy-start | bytes 12582916
  440.9 1.1 copy-start.12
  464.3 22.7 %copy-start.9 = (bf16[32,4096]{1,0:T(8,128)(2,1)S(1)}, bf16[32,4096]{1,0:T(8,128)(2,1)}, u32[]{:S(2)}) copy-start(bf16[32,4096]{1,0:T(8,128)(2,1)} %copy-done.8) | copy-start | bytes 786436
  464.3 22.7 %copy-start.11 = (bf16[32,4096]{1,0:T(8,128)(2,1)S(1)}, bf16[32,4096]{1,0:T(8,128)(2,1)}, u32[]{:S(2)}) copy-start(bf16[32,4096]{1,0:T(8,128)(2,1)} %copy-done.10) | copy-start | bytes 786436
  487.3 1.0 copy-start.2
  487.3 1.3 copy-start.5
Sparse Core Ops, SparseCore 0:
  67.6 21.6 reduce-scatter.5
  150.4 20.3 reduce-scatter.7
  270.6 19.4 reduce-scatter.9
  390.6 19.2 reduce-scatter.11
  465.5 20.3 reduce-scatter.13
where the time goes:
time: 505 us; the launch traced here: 496 us
  waiting for transfers between devices  169 us (33%)
  matrix products  152 us (30%)
  blocking collectives  85.7 us (17%)
  other arithmetic  37.4 us (7%)
  starting transfers between devices  22.2 us (4%)
  between operations  15.3 us (3%)
  local copies, waits for them, and re-layouts  13.8 us (3%)
    reduce_scatter x5, waiting for transfers between devices, section_layer(): lax.psum_scatter(jnp.concatenate([term_mem, term_seg], axis=1).reshape(bl...  90.2 us
    all_to_all x2, waiting for transfers between devices, route_memory(): lax.all_to_all(outgoing, 'dp', split_axis=0, concat_axis=0, tiled=True)  73.2 us
    all_gather x5, blocking collectives, section_layer(): lax.all_gather(seg_x, 'mp', axis=0, tiled=True)  45.2 us
    dot_general x5, matrix products, section_layer(): jnp.dot(attended_seg, w_out, preferred_element_type=jnp.float32)  44.1 us
    dot_general x5, matrix products, section_layer(): jnp.dot(attended_mem, w_out, preferred_element_type=jnp.float32)  44 us
    dot_general x5, matrix products, section_layer(): jnp.dot(normed, w_query, preferred_element_type=jnp.float32)  41.3 us
    all_gather x5, blocking collectives, section_layer(): lax.all_gather(mem_x, 'mp', axis=0, tiled=True)  40.5 us
    all_to_all x2, starting transfers between devices, route_memory(): lax.all_to_all(outgoing, 'dp', split_axis=0, concat_axis=0, tiled=True)  11 us
  transfers between devices with their start and end apart: 15, of which 12 were waited for; matrix products, arithmetic and copies ran while one was open for 2% of the time, Pallas kernels for 0%

commit v1 on v0

--- a/solution.py
+++ b/solution.py
@@ -5,6 +5,18 @@
 
 HEAD_SIZE = 128
 EPSILON = 1e-05
+
+
+def collect(value, axis, dim):
+    ways, here = (lax.axis_size(axis), lax.axis_index(axis))
+    grown, reach = (value, 1)
+    while reach < ways:
+        theirs = lax.ppermute(grown, axis, [(d, d ^ reach) for d in range(ways)])
+        mine_first = jnp.concatenate([grown, theirs], axis=dim)
+        theirs_first = jnp.concatenate([theirs, grown], axis=dim)
+        grown = jnp.where(here & reach == 0, mine_first, theirs_first)
+        reach = 2 * reach
+    return grown
 
 
 def shifted(value, axis, steps):
@@ -22,10 +34,7 @@
 def section_layer(mem_x, seg_x, length, w_query, w_key, value_weight, w_out, gain):
     mem_dev = mem_x.shape[0]
     seg_dev = seg_x.shape[0]
-    raw_mem, raw_seg = (
-        lax.all_gather(mem_x, "mp", axis=0, tiled=True),
-        lax.all_gather(seg_x, "mp", axis=0, tiled=True),
-    )
+    raw_mem, raw_seg = (lax.all_gather(mem_x, "mp", axis=0, tiled=True), collect(seg_x, "mp", 0))
     all_mem = norm_rows(raw_mem, gain)
     all_seg = norm_rows(raw_seg, gain)
     mem_rows = all_mem.shape[0]

time: 505 us -> 521 us (1.032)
  blocking collectives: 85.7 us -> 45.2 us
  waiting for transfers between devices: 169 us -> 197 us
  local copies, waits for them, and re-layouts: 13.8 us -> 24.3 us
  matrix products: 152 us -> 159 us
  other arithmetic: 37.4 us -> 43.3 us
    all_gather x5 -> x0, blocking collectives: 45.2 us -> none  [section_layer(): lax.all_gather(seg_x, 'mp', axis=0, tiled=True)]
    ppermute x0 -> x5, waiting for transfers between devices: none -> 29.3 us  [collect(): theirs = lax.ppermute(grown, axis, [(d, d ^ reach) for d in range(ways)])]
    unnamed x50 -> x54, local copies, waits for them, and re-layouts: 2.12 us -> 9.56 us
  transfers between devices with their start and end apart: 15 -> 20, of which waited for: 12 -> 15; matrix products, arithmetic and copies ran while one was open for 2% -> 3% of each run, Pallas kernels for 0% -> 0%
where the time goes in v1:
time: 521 us; the launch traced here: 511 us
  waiting for transfers between devices  197 us (38%)
  matrix products  159 us (31%)
  blocking collectives  45.2 us (9%)
  other arithmetic  43.3 us (8%)
  starting transfers between devices  27.1 us (5%)
  local copies, waits for them, and re-layouts  24.3 us (5%)
  between operations  15.1 us (3%)
    reduce_scatter x5, waiting for transfers between devices, section_layer(): lax.psum_scatter(jnp.concatenate([term_mem, term_seg], axis=1).reshape(bl...  89.4 us
    all_to_all x2, waiting for transfers between devices, route_memory(): lax.all_to_all(outgoing, 'dp', split_axis=0, concat_axis=0, tiled=True)  73.8 us
    all_gather x5, blocking collectives, section_layer(): lax.all_gather(mem_x, 'mp', axis=0, tiled=True)  45.2 us
    dot_general x5, matrix products, section_layer(): jnp.dot(attended_mem, w_out, preferred_element_type=jnp.float32)  44.1 us
    dot_general x5, matrix products, section_layer(): jnp.dot(attended_seg, w_out, preferred_element_type=jnp.float32)  44 us
    dot_general x5, matrix products, section_layer(): jnp.dot(normed, w_query, preferred_element_type=jnp.float32)  41.2 us
    ppermute x5, waiting for transfers between devices, collect(): theirs = lax.ppermute(grown, axis, [(d, d ^ reach) for d in range(ways)])  29.3 us
    all_to_all x2, starting transfers between devices, route_memory(): lax.all_to_all(outgoing, 'dp', split_axis=0, concat_axis=0, tiled=True)  11 us
  transfers between devices with their start and end apart: 20, of which 15 were waited for; matrix products, arithmetic and copies ran while one was open for 3% of the time, Pallas kernels for 0%

profile of v1, /device:TPU:0, one launch (start us, length us, event | category | flops | bytes accessed | tf_op | source)
XLA Modules:
  0.0 511.0 jit_solution(3795206162003100466)
XLA Ops:
  8.2 3.0 collective-permute-start
  12.2 10.9 %all-gather = bf16[1,64,4096]{2,1,0:T(8,128)(2,1)S(1)} all-gather(bf16[1,32,4096]{2,1,0:T(8,128)(2,1)S(1)} %slice_select_fusion), channel_id=2, replica_groups=mesh['phase'=2,'dp'=8,'mp'=2] {'mp'}, dimensions={1}, use_global_device_ids=true | all-gather | bytes 786432 | tf_op jit(solution)/shard_map/all_gather | solution.py:37
  30.2 8.1 %fusion.85 = bf16[128,2048]{1,0:T(8,128)(2,1)S(1)} fusion(bf16[1,4096,2048]{2,1,0:T(8,128)(2,1)} %param.13, bf16[64,4096]{1,0:T(8,128)(2,1)S(1)} %get-tuple-element.52, bf16[64,4096]{1,0:T(8,128)(2,1)S(1)} %get-tuple-element.51), kind=kOutput, calls=%fused_computation.65 | convolution fusion | flops 2149842944 | bytes 18350080 | tf_op jit(solution)/shard_map/dot_general | solution.py:46
  38.7 2.9 fusion.140
  42.5 2.9 fusion.125
  46.7 8.8 %fusion.38 = bf16[2,32,4096]{2,1,0:T(8,128)(2,1)S(1)} fusion(bf16[2,32,2048]{2,1,0:T(8,128)(2,1)S(1)} %dot_general.132, bf16[1,2048,4096]{2,1,0:T(8,128)(2,1)} %param.16), kind=kOutput, calls=%fused_computation.36 | convolution fusion | flops 1074003968 | bytes 17563648 | tf_op jit(solution)/shard_map/dot_general | solution.py:79
  55.5 8.8 %fusion.35 = bf16[2,32,4096]{2,1,0:T(8,128)(2,1)S(1)} fusion(bf16[2,32,2048]{2,1,0:T(8,128)(2,1)S(1)} %dot_general.130, bf16[1,2048,4096]{2,1,0:T(8,128)(2,1)} %param.16), kind=kOutput, calls=%fused_computation.35 | convolution fusion | flops 1074003968 | bytes 17563648 | tf_op jit(solution)/shard_map/dot_general | solution.py:76
  65.4 9.3 %reduce-scatter.8.cloned.1.call-start = ((), (), s32[]{:S(2)}) async-start(), calls=%async_computation.8 | async-start | bytes 1572864 | tf_op jit(solution)/shard_map/reduce_scatter | solution.py:82
  74.7 12.7 %reduce-scatter.6.cloned.1.call-done = bf16[64,4096]{1,0:T(8,128)(2,1)} async-done(((bf16[128,4096]{1,0:T(8,128)(2,1)}), bf16[64,4096]{1,0:T(8,128)(2,1)}) %reduce-scatter.6.cloned.1.call-update) | async-done | bytes 524304 | tf_op jit(solution)/shard_map/reduce_scatter | solution.py:82
  90.6 8.9 %all_gather.16 = bf16[64,4096]{1,0:T(8,128)(2,1)S(1)} all-gather(bf16[32,4096]{1,0:T(8,128)(2,1)S(1)} %bitcast_select_fusion.9), channel_id=1, replica_groups=mesh['phase'=2,'dp'=8,'mp'=2] {'mp'}, dimensions={0}, use_global_device_ids=true | all-gather | bytes 786432 | tf_op jit(solution)/shard_map/all_gather | solution.py:37
  101.1 6.8 %collective-permute-done.3 = bf16[32,4096]{1,0:T(8,128)(2,1)S(1)} collective-permute-done((bf16[32,4096]{1,0:T(8,128)(2,1)S(1)}, bf16[32,4096]{1,0:T(8,128)(2,1)S(1)}, u32[]{:S(2)}, u32[]{:S(2)}) %collective-permute-start.3) | collective-permute-done | bytes 262176 | tf_op jit(solution)/shard_map/ppermute | solution.py:14
  108.5 8.3 %fusion.88 = bf16[128,2048]{1,0:T(8,128)(2,1)S(1)} fusion(bf16[1,4096,2048]{2,1,0:T(8,128)(2,1)} %param.13, bf16[64,4096]{1,0:T(8,128)(2,1)S(1)} %get-tuple-element.50, bf16[64,4096]{1,0:T(8,128)(2,1)S(1)} %get-tuple-element.49), kind=kOutput, calls=%fused_computation.66 | convolution fusion | flops 2149842944 | bytes 18350080 | tf_op jit(solution)/shard_map/dot_general | solution.py:46
  121.0 1.5 fusion.307
  122.6 2.3 fusion.117
  124.9 2.8 fusion.121
  127.7 1.8 fusion.300
  129.9 8.8 %fusion.44 = bf16[2,32,4096]{2,1,0:T(8,128)(2,1)S(1)} fusion(bf16[2,32,2048]{2,1,0:T(8,128)(2,1)S(1)} %dot_general.141, bf16[1,2048,4096]{2,1,0:T(8,128)(2,1)} %param.16), kind=kOutput, calls=%fused_computation.38 | convolution fusion | flops 1074003968 | bytes 17563648 | tf_op jit(solution)/shard_map/dot_general | solution.py:79
  140.8 8.8 %fusion.41 = bf16[2,32,4096]{2,1,0:T(8,128)(2,1)S(1)} fusion(bf16[2,32,2048]{2,1,0:T(8,128)(2,1)S(1)} %dot_general.139, bf16[1,2048,4096]{2,1,0:T(8,128)(2,1)} %param.16), kind=kOutput, calls=%fused_computation.37 | convolution fusion | flops 1074003968 | bytes 17563648 | tf_op jit(solution)/shard_map/dot_general | solution.py:76
  150.8 20.5 %reduce-scatter.8.cloned.1.call-done = bf16[64,4096]{1,0:T(8,128)(2,1)} async-done(((bf16[128,4096]{1,0:T(8,128)(2,1)}), bf16[64,4096]{1,0:T(8,128)(2,1)}) %reduce-scatter.8.cloned.1.call-update) | async-done | bytes 524304 | tf_op jit(solution)/shard_map/reduce_scatter | solution.py:82
  175.2 1.6 broadcast_select_fusion.1
  176.7 5.5 %all-to-all-start = ((bf16[8,32,4096]{2,1,0:T(8,128)(2,1)}), bf16[8,32,4096]{2,1,0:T(8,128)(2,1)S(1)}, u32[]{:S(2)}, u32[]{:S(2)}) async-start(bf16[8,32,4096]{2,1,0:T(8,128)(2,1)} %broadcast_select_fusion.1), calls=%async_computation.2 | async-start | bytes 4194304 | tf_op jit(solution)/shard_map/all_to_all | solution.py:102
  185.5 7.8 %collective-permute-done.6 = bf16[32,4096]{1,0:T(8,128)(2,1)S(1)} collective-permute-done((bf16[32,4096]{1,0:T(8,128)(2,1)S(1)}, bf16[32,4096]{1,0:T(8,128)(2,1)S(1)}, u32[]{:S(2)}, u32[]{:S(2)}) %collective-permute-start.6) | collective-permute-done | bytes 262176 | tf_op jit(solution)/shard_map/ppermute | solution.py:14
  194.1 37.1 %all-to-all-done = bf16[8,32,4096]{2,1,0:T(8,128)(2,1)S(1)} async-done(((bf16[8,32,4096]{2,1,0:T(8,128)(2,1)}), bf16[8,32,4096]{2,1,0:T(8,128)(2,1)S(1)}, u32[]{:S(2)}, u32[]{:S(2)}) %all-to-all-start) | async-done | bytes 2097184 | tf_op jit(solution)/shard_map/all_to_all | solution.py:102
  233.2 8.2 %all_gather.17 = bf16[64,4096]{1,0:T(8,128)(2,1)S(1)} all-gather(bf16[32,4096]{1,0:T(8,128)(2,1)S(1)} %broadcast_select_fusion.5), channel_id=1, replica_groups=mesh['phase'=2,'dp'=8,'mp'=2] {'mp'}, dimensions={0}, use_global_device_ids=true | all-gather | bytes 786432 | tf_op jit(solution)/shard_map/all_gather | solution.py:37
  243.0 8.3 %fusion.91 = bf16[128,2048]{1,0:T(8,128)(2,1)S(1)} fusion(bf16[1,4096,2048]{2,1,0:T(8,128)(2,1)} %param.13, bf16[64,4096]{1,0:T(8,128)(2,1)S(1)} %get-tuple-element.48, bf16[64,4096]{1,0:T(8,128)(2,1)S(1)} %get-tuple-element.47), kind=kOutput, calls=%fused_computation.67 | convolution fusion | flops 2149842944 | bytes 18350080 | tf_op jit(solution)/shard_map/dot_general | solution.py:46
  252.0 1.5 copy-done.24
  256.5 2.0 fusion.122
  258.9 8.8 %fusion.50 = bf16[2,32,4096]{2,1,0:T(8,128)(2,1)S(1)} fusion(bf16[2,32,2048]{2,1,0:T(8,128)(2,1)S(1)} %dot_general.150, bf16[1,2048,4096]{2,1,0:T(8,128)(2,1)} %param.16), kind=kOutput, calls=%fused_computation.40 | convolution fusion | flops 1074003968 | bytes 17563648 | tf_op jit(solution)/shard_map/dot_general | solution.py:79
  268.1 8.8 %fusion.47 = bf16[2,32,4096]{2,1,0:T(8,128)(2,1)S(1)} fusion(bf16[2,32,2048]{2,1,0:T(8,128)(2,1)S(1)} %dot_general.148, bf16[1,2048,4096]{2,1,0:T(8,128)(2,1)} %param.16), kind=kOutput, calls=%fused_computation.39 | convolution fusion | flops 1074003968 | bytes 17563648 | tf_op jit(solution)/shard_map/dot_general | solution.py:76
  279.0 18.4 %reduce-scatter.10.cloned.1.call-done = bf16[64,4096]{1,0:T(8,128)(2,1)} async-done(((bf16[128,4096]{1,0:T(8,128)(2,1)}), bf16[64,4096]{1,0:T(8,128)(2,1)}) %reduce-scatter.10.cloned.1.call-update) | async-done | bytes 524304 | tf_op jit(solution)/shard_map/reduce_scatter | solution.py:82
  301.7 1.6 broadcast_select_fusion
  303.3 5.5 %all-to-all-start.1 = ((bf16[8,32,4096]{2,1,0:T(8,128)(2,1)}), bf16[8,32,4096]{2,1,0:T(8,128)(2,1)S(1)}, u32[]{:S(2)}, u32[]{:S(2)}) async-start(bf16[8,32,4096]{2,1,0:T(8,128)(2,1)} %broadcast_select_fusion), calls=%async_computation.4 | async-start | bytes 4194304 | tf_op jit(solution)/shard_map/all_to_all | solution.py:102
  309.0 1.5 collective-permute-done.8
  312.1 7.8 %collective-permute-done.9 = bf16[32,4096]{1,0:T(8,128)(2,1)S(1)} collective-permute-done((bf16[32,4096]{1,0:T(8,128)(2,1)S(1)}, bf16[32,4096]{1,0:T(8,128)(2,1)S(1)}, u32[]{:S(2)}, u32[]{:S(2)}) %collective-permute-start.9) | collective-permute-done | bytes 262176 | tf_op jit(solution)/shard_map/ppermute | solution.py:14
  320.6 36.8 %all-to-all-done.1 = bf16[8,32,4096]{2,1,0:T(8,128)(2,1)S(1)} async-done(((bf16[8,32,4096]{2,1,0:T(8,128)(2,1)}), bf16[8,32,4096]{2,1,0:T(8,128)(2,1)S(1)}, u32[]{:S(2)}, u32[]{:S(2)}) %all-to-all-start.1) | async-done | bytes 2097184 | tf_op jit(solution)/shard_map/all_to_all | solution.py:102
  360.1 7.9 %all_gather.18 = bf16[64,4096]{1,0:T(8,128)(2,1)S(1)} all-gather(bf16[32,4096]{1,0:T(8,128)(2,1)S(1)} %broadcast_select_fusion.4), channel_id=1, replica_groups=mesh['phase'=2,'dp'=8,'mp'=2] {'mp'}, dimensions={0}, use_global_device_ids=true | all-gather | bytes 786432 | tf_op jit(solution)/shard_map/all_gather | solution.py:37
  369.6 8.3 %fusion.94 = bf16[128,2048]{1,0:T(8,128)(2,1)S(1)} fusion(bf16[1,4096,2048]{2,1,0:T(8,128)(2,1)} %param.13, bf16[64,4096]{1,0:T(8,128)(2,1)S(1)} %get-tuple-element.46, bf16[64,4096]{1,0:T(8,128)(2,1)S(1)} %get-tuple-element.45), kind=kOutput, calls=%fused_computation.68 | convolution fusion | flops 2149842944 | bytes 18350080 | tf_op jit(solution)/shard_map/dot_general | solution.py:46
  383.8 8.8 %fusion.56 = bf16[2,32,4096]{2,1,0:T(8,128)(2,1)S(1)} fusion(bf16[2,32,2048]{2,1,0:T(8,128)(2,1)S(1)} %dot_general.159, bf16[1,2048,4096]{2,1,0:T(8,128)(2,1)} %param.16), kind=kOutput, calls=%fused_computation.42 | convolution fusion | flops 1074003968 | bytes 17563648 | tf_op jit(solution)/shard_map/dot_general | solution.py:79
  393.7 9.0 %fusion.53 = bf16[2,32,4096]{2,1,0:T(8,128)(2,1)S(1)} fusion(bf16[2,32,2048]{2,1,0:T(8,128)(2,1)} %dot_general.157, bf16[1,2048,4096]{2,1,0:T(8,128)(2,1)} %param.16), kind=kOutput, calls=%fused_computation.41 | convolution fusion | flops 1074003968 | bytes 17563648 | tf_op jit(solution)/shard_map/dot_general | solution.py:76
  405.2 18.1 %reduce-scatter.12.cloned.1.call-done = bf16[64,4096]{1,0:T(8,128)(2,1)} async-done(((bf16[128,4096]{1,0:T(8,128)(2,1)}), bf16[64,4096]{1,0:T(8,128)(2,1)}) %reduce-scatter.12.cloned.1.call-update) | async-done | bytes 524304 | tf_op jit(solution)/shard_map/reduce_scatter | solution.py:82
  427.4 9.2 %all_gather.19 = bf16[64,4096]{1,0:T(8,128)(2,1)S(1)} all-gather(bf16[32,4096]{1,0:T(8,128)(2,1)S(1)} %broadcast_select_fusion.3), channel_id=1, replica_groups=mesh['phase'=2,'dp'=8,'mp'=2] {'mp'}, dimensions={0}, use_global_device_ids=true | all-gather | bytes 786432 | tf_op jit(solution)/shard_map/all_gather | solution.py:37
  437.3 6.9 %collective-permute-done.12 = bf16[32,4096]{1,0:T(8,128)(2,1)S(1)} collective-permute-done((bf16[32,4096]{1,0:T(8,128)(2,1)S(1)}, bf16[32,4096]{1,0:T(8,128)(2,1)S(1)}, u32[]{:S(2)}, u32[]{:S(2)}) %collective-permute-start.12) | collective-permute-done | bytes 262176 | tf_op jit(solution)/shard_map/ppermute | solution.py:14
  444.8 8.3 %fusion.97 = bf16[128,2048]{1,0:T(8,128)(2,1)S(1)} fusion(bf16[1,4096,2048]{2,1,0:T(8,128)(2,1)} %param.13, bf16[64,4096]{1,0:T(8,128)(2,1)S(1)} %get-tuple-element.44, bf16[64,4096]{1,0:T(8,128)(2,1)S(1)} %get-tuple-element.43), kind=kOutput, calls=%fused_computation.69 | convolution fusion | flops 2149842944 | bytes 18350080 | tf_op jit(solution)/shard_map/dot_general | solution.py:46
  453.9 1.5 copy-done.26
  458.3 2.0 fusion.124
  460.8 8.8 %fusion.62 = bf16[2,32,4096]{2,1,0:T(8,128)(2,1)S(1)} fusion(bf16[2,32,2048]{2,1,0:T(8,128)(2,1)S(1)} %dot_general.168, bf16[1,2048,4096]{2,1,0:T(8,128)(2,1)} %param.16), kind=kOutput, calls=%fused_computation.44 | convolution fusion | flops 1074003968 | bytes 17563648 | tf_op jit(solution)/shard_map/dot_general | solution.py:79
  470.0 8.8 %fusion.59 = bf16[2,32,4096]{2,1,0:T(8,128)(2,1)S(1)} fusion(bf16[2,32,2048]{2,1,0:T(8,128)(2,1)S(1)} %dot_general.166, bf16[1,2048,4096]{2,1,0:T(8,128)(2,1)} %param.16), kind=kOutput, calls=%fused_computation.43 | convolution fusion | flops 1074003968 | bytes 17563648 | tf_op jit(solution)/shard_map/dot_general | solution.py:76
  480.7 19.7 %reduce-scatter.14.cloned.1.call-done = bf16[64,4096]{1,0:T(8,128)(2,1)} async-done(((bf16[128,4096]{1,0:T(8,128)(2,1)}), bf16[64,4096]{1,0:T(8,128)(2,1)}) %reduce-scatter.14.cloned.1.call-update) | async-done | bytes 524304 | tf_op jit(solution)/shard_map/reduce_scatter | solution.py:82
  (212 shorter events, 79.6 us)
Async XLA Ops:
  7.2 80.2 %reduce-scatter.6.cloned.1.call-start = ((), (), s32[]{:S(2)}) async-start(), calls=%async_computation.7 | async-start | bytes 1572864 | tf_op jit(solution)/shard_map/reduce_scatter | solution.py:82
  8.2 21.4 %collective-permute-start = (bf16[32,4096]{1,0:T(8,128)(2,1)S(1)}, bf16[32,4096]{1,0:T(8,128)(2,1)S(1)}, u32[]{:S(2)}, u32[]{:S(2)}) collective-permute-start(bf16[32,4096]{1,0:T(8,128)(2,1)S(1)} %select_bitcast_fusion), channel_id=1, source_target_pairs={{0,1},{1,0},{2,3},{3,2},{4,5},{5,4},{6,7},{7,6},{8,9},{9,8},{10,11... | collective-permute-start | bytes 786440 | tf_op jit(solution)/shard_map/ppermute | solution.py:14
  64.3 24.3 %copy-start.5 = (bf16[2,32,4096]{2,1,0:T(8,128)(2,1)S(1)}, bf16[2,32,4096]{2,1,0:T(8,128)(2,1)}, u32[]{:S(2)}) copy-start(bf16[2,32,4096]{2,1,0:T(8,128)(2,1)} %param.10) | copy-start | bytes 1572868
  65.4 105.9 %reduce-scatter.8.cloned.1.call-start = ((), (), s32[]{:S(2)}) async-start(), calls=%async_computation.8 | async-start | bytes 1572864 | tf_op jit(solution)/shard_map/reduce_scatter | solution.py:82
  88.7 1.8 collective-permute-start.1
  90.0 9.5 %collective-permute-start.2 = (bf16[32,4096]{1,0:T(8,128)(2,1)S(1)}, bf16[32,4096]{1,0:T(8,128)(2,1)S(1)}, u32[]{:S(2)}, u32[]{:S(2)}) collective-permute-start(bf16[32,4096]{1,0:T(8,128)(2,1)S(1)} %get-tuple-element.16), channel_id=1, source_target_pairs={{0,16},{16,0},{1,17},{17,1},{2,18},{18,2},{3,19},{19,3},{4,20},{20... | collective-permute-start | bytes 786440 | tf_op jit(solution)/shard_map/ppermute | solution.py:25
  100.5 7.4 %collective-permute-start.3 = (bf16[32,4096]{1,0:T(8,128)(2,1)S(1)}, bf16[32,4096]{1,0:T(8,128)(2,1)S(1)}, u32[]{:S(2)}, u32[]{:S(2)}) collective-permute-start(bf16[32,4096]{1,0:T(8,128)(2,1)S(1)} %bitcast_select_fusion.8), channel_id=1, source_target_pairs={{0,1},{1,0},{2,3},{3,2},{4,5},{5,4},{6,7},{7,6},{8,9},{9,8},{10,11... | collective-permute-start | bytes 786440 | tf_op jit(solution)/shard_map/ppermute | solution.py:14
  108.5 8.4 %copy-start.19 = (bf16[1,4096,512]{2,1,0:T(8,128)(2,1)S(1)}, bf16[1,4096,512]{2,1,0:T(8,128)(2,1)}, u32[]{:S(2)}) copy-start(bf16[1,4096,512]{2,1,0:T(8,128)(2,1)} %param.14) | copy-start | bytes 12582916
  116.9 2.2 copy-start.23
  129.9 8.9 %copy-start.10 = (bf16[64,4,4,128]{3,0,2,1:T(8,128)(2,1)S(1)}, bf16[64,4,4,128]{3,0,2,1:T(8,128)(2,1)}, u32[]{:S(2)}) copy-start(bf16[64,4,4,128]{3,0,2,1:T(8,128)(2,1)} %get-tuple-element.39) | copy-start | bytes 786436
  149.6 23.7 %copy-start.18 = (s32[2,8]{1,0:T(2,128)S(1)}, s32[2,8]{1,0:T(2,128)}, u32[]{:S(2)}) copy-start(s32[2,8]{1,0:T(2,128)} %param.12) | copy-start | bytes 196
  173.3 3.4 copy-start.1
  173.3 1.8 collective-permute-start.4
  175.1 1.6 copy-start.8
  176.7 54.4 %all-to-all-start = ((bf16[8,32,4096]{2,1,0:T(8,128)(2,1)}), bf16[8,32,4096]{2,1,0:T(8,128)(2,1)S(1)}, u32[]{:S(2)}, u32[]{:S(2)}) async-start(bf16[8,32,4096]{2,1,0:T(8,128)(2,1)} %broadcast_select_fusion.1), calls=%async_computation.2 | async-start | bytes 4194304 | tf_op jit(solution)/shard_map/all_to_all | solution.py:102
  182.2 115.1 %reduce-scatter.10.cloned.1.call-start = ((), (), s32[]{:S(2)}) async-start(), calls=%async_computation.9 | async-start | bytes 1572864 | tf_op jit(solution)/shard_map/reduce_scatter | solution.py:82
  182.3 1.6 collective-permute-start.5
  184.9 8.5 %collective-permute-start.6 = (bf16[32,4096]{1,0:T(8,128)(2,1)S(1)}, bf16[32,4096]{1,0:T(8,128)(2,1)S(1)}, u32[]{:S(2)}, u32[]{:S(2)}) collective-permute-start(bf16[32,4096]{1,0:T(8,128)(2,1)S(1)} %bitcast_select_fusion.6), channel_id=1, source_target_pairs={{0,1},{1,0},{2,3},{3,2},{4,5},{5,4},{6,7},{7,6},{8,9},{9,8},{10,11... | collective-permute-start | bytes 786440 | tf_op jit(solution)/shard_map/ppermute | solution.py:14
  193.4 0.7 copy-start.7
  243.0 8.3 %copy-start.20 = (bf16[1,4096,512]{2,1,0:T(8,128)(2,1)S(1)}, bf16[1,4096,512]{2,1,0:T(8,128)(2,1)}, u32[]{:S(2)}) copy-start(bf16[1,4096,512]{2,1,0:T(8,128)(2,1)} %param.14) | copy-start | bytes 12582916
  251.3 2.2 copy-start.24
  253.5 1.2 copy-start.17
  299.5 9.4 %copy-start.14 = (bf16[32,4096]{1,0:T(8,128)(2,1)S(1)}, bf16[32,4096]{1,0:T(8,128)(2,1)}, u32[]{:S(2)}) copy-start(bf16[32,4096]{1,0:T(8,128)(2,1)} %get-tuple-element.12) | copy-start | bytes 786436
  299.5 1.5 collective-permute-start.7
  301.0 0.7 copy-start.9
  303.3 54.1 %all-to-all-start.1 = ((bf16[8,32,4096]{2,1,0:T(8,128)(2,1)}), bf16[8,32,4096]{2,1,0:T(8,128)(2,1)S(1)}, u32[]{:S(2)}, u32[]{:S(2)}) async-start(bf16[8,32,4096]{2,1,0:T(8,128)(2,1)} %broadcast_select_fusion), calls=%async_computation.4 | async-start | bytes 4194304 | tf_op jit(solution)/shard_map/all_to_all | solution.py:102
  308.8 114.5 %reduce-scatter.12.cloned.1.call-start = ((), (), s32[]{:S(2)}) async-start(), calls=%async_computation.10 | async-start | bytes 1572864 | tf_op jit(solution)/shard_map/reduce_scatter | solution.py:82
  308.9 1.6 collective-permute-start.8
  311.5 8.4 %collective-permute-start.9 = (bf16[32,4096]{1,0:T(8,128)(2,1)S(1)}, bf16[32,4096]{1,0:T(8,128)(2,1)S(1)}, u32[]{:S(2)}, u32[]{:S(2)}) collective-permute-start(bf16[32,4096]{1,0:T(8,128)(2,1)S(1)} %bitcast_select_fusion.4), channel_id=1, source_target_pairs={{0,1},{1,0},{2,3},{3,2},{4,5},{5,4},{6,7},{7,6},{8,9},{9,8},{10,11... | collective-permute-start | bytes 786440 | tf_op jit(solution)/shard_map/ppermute | solution.py:14
  319.9 0.7 copy-start.6
  359.4 0.7 copy-start.4
  369.6 8.3 %copy-start.21 = (bf16[1,4096,512]{2,1,0:T(8,128)(2,1)S(1)}, bf16[1,4096,512]{2,1,0:T(8,128)(2,1)}, u32[]{:S(2)}) copy-start(bf16[1,4096,512]{2,1,0:T(8,128)(2,1)} %param.14) | copy-start | bytes 12582916
  377.9 2.2 copy-start.25
  380.1 1.2 copy-start.16
  393.7 10.8 %copy-start.2 = (bf16[4,32,4096]{2,1,0:T(8,128)(2,1)S(1)}, bf16[4,32,4096]{2,1,0:T(8,128)(2,1)}, u32[]{:S(2)}) copy-start(bf16[4,32,4096]{2,1,0:T(8,128)(2,1)} %get-tuple-element.29) | copy-start | bytes 3145732
  403.7 96.7 %reduce-scatter.14.cloned.1.call-start = ((), (), s32[]{:S(2)}) async-start(), calls=%async_computation.11 | async-start | bytes 1572864 | tf_op jit(solution)/shard_map/reduce_scatter | solution.py:82
  425.8 1.6 collective-permute-start.10
  425.8 10.8 %collective-permute-start.11 = (bf16[32,4096]{1,0:T(8,128)(2,1)S(1)}, bf16[32,4096]{1,0:T(8,128)(2,1)S(1)}, u32[]{:S(2)}, u32[]{:S(2)}) collective-permute-start(bf16[32,4096]{1,0:T(8,128)(2,1)S(1)} %get-tuple-element.10), channel_id=1, source_target_pairs={{0,16},{16,0},{1,17},{17,1},{2,18},{18,2},{3,19},{19,3},{4,20},{20... | collective-permute-start | bytes 786440 | tf_op jit(solution)/shard_map/ppermute | solution.py:25
  427.4 9.3 %copy-start.11 = (bf16[32,4096]{1,0:T(8,128)(2,1)}, bf16[32,4096]{1,0:T(8,128)(2,1)S(1)}, u32[]{:S(2)}) copy-start(bf16[32,4096]{1,0:T(8,128)(2,1)S(1)} %collective-permute-done.10) | copy-start | bytes 786436
  436.6 7.8 %copy-start.13 = (bf16[32,4096]{1,0:T(8,128)(2,1)}, bf16[32,4096]{1,0:T(8,128)(2,1)S(1)}, u32[]{:S(2)}) copy-start(bf16[32,4096]{1,0:T(8,128)(2,1)S(1)} %collective-permute-done.11) | copy-start | bytes 786436
  436.7 7.6 %collective-permute-start.12 = (bf16[32,4096]{1,0:T(8,128)(2,1)S(1)}, bf16[32,4096]{1,0:T(8,128)(2,1)S(1)}, u32[]{:S(2)}, u32[]{:S(2)}) collective-permute-start(bf16[32,4096]{1,0:T(8,128)(2,1)S(1)} %broadcast_select_fusion.2), channel_id=1, source_target_pairs={{0,1},{1,0},{2,3},{3,2},{4,5},{5,4},{6,7},{7,6},{8,9},{9,8},{10,11... | collective-permute-start | bytes 786440 | tf_op jit(solution)/shard_map/ppermute | solution.py:14
  444.8 8.3 %copy-start.22 = (bf16[1,4096,512]{2,1,0:T(8,128)(2,1)S(1)}, bf16[1,4096,512]{2,1,0:T(8,128)(2,1)}, u32[]{:S(2)}) copy-start(bf16[1,4096,512]{2,1,0:T(8,128)(2,1)} %param.14) | copy-start | bytes 12582916
  453.1 2.2 copy-start.26
  455.3 1.2 copy-start.15
  478.8 22.8 %copy-start.12 = (bf16[32,4096]{1,0:T(8,128)(2,1)S(1)}, bf16[32,4096]{1,0:T(8,128)(2,1)}, u32[]{:S(2)}) copy-start(bf16[32,4096]{1,0:T(8,128)(2,1)} %copy-done.11) | copy-start | bytes 786436
  502.8 1.0 copy-start
  502.8 1.3 copy-start.3
Sparse Core Ops, SparseCore 0:
  65.5 21.8 reduce-scatter.5
  150.8 20.3 reduce-scatter.7
  278.1 19.2 reduce-scatter.9
  403.8 19.4 reduce-scatter.11
  480.0 20.3 reduce-scatter.13
